TPU v7x, 128 devices: a whole 4x4x4 slice. The times are simulated.
128 devices in a mesh: row: 8 (over z, core), col: 16 (over x, y).
Axes of the slice: x: 4, y: 4, z: 4, core: 2. Of those that a mesh axis runs over, the one named last changes fastest.
Arguments:
- normed: bfloat16 [8192, 7168], P(None, 'col'), may hold values from -44 to 44
- projection_weight: bfloat16 [7168, 3, 7168], P('col', None, 'row')
- adapter_down_weight: bfloat16 [7168, 16, 32], P(None, 'col'), may hold values from -0.0625 to 0.0625
- adapter_up_weight: bfloat16 [16, 2, 16, 7168], P(None, None, None, 'row'), may hold values from -0.47851562 to 0.47851562
- packed_prompt_length: int32 [64], replicated, may hold values from 64 to 512, as said below
- prompt_adapter_ids: int32 [64], replicated, may hold values from 0 to 63, as said below
- slot_adapter_ids: int32 [16], replicated, may hold values from 0 to 63, as said below
- prompt_page_slots: int32 [64, 4], replicated, may hold values from -1 to 159, as said below
Outputs:
- attended: bfloat16 [8192, 7168], P('col', 'row')
- kv_cache: bfloat16 [160, 128, 2, 7168], P('col', None, None, 'row')
Inputs may be any that keep to these rules, and one draw needn't show every extreme that they name: `packed_prompt_length`: the 64 lengths sum to 8192; one of them is exactly 512 and one exactly 64. `slot_adapter_ids`: distinct adapter ids. `prompt_adapter_ids`: every entry is one of slot_adapter_ids, and every loaded adapter is named by at least one prompt. `prompt_page_slots`: entry [i, j] is -1 where 128 * j >= packed_prompt_length[i]; otherwise it lies among slots 10 * c to 10 * c + 9, where c is the block of 512 packed tokens that holds the page's last token. No slot is named twice.
All inputs are finite; a program needn't handle non-finite values.
Results may differ from a plain program's by a relative error of at most 0.0072.
Values may be sent and summed in bfloat16 or wider, within the bound.
A program may use at most 256 MiB of HBM per device.

v0:
```python
import jax
import jax.numpy as jnp
from jax import lax
from jax.sharding import PartitionSpec as P

HEAD_DIM = 128
PAGE = 128
NEAR = 1
SLOTS_DEV = 10
adapter_scale = 2.0
masked_score = -1e30


def shifted(block, axis, distance):
    devices = range(lax.axis_size(axis))
    route = [(i - distance, i) for i in devices if i - distance in devices]
    return lax.ppermute(block, axis, route)


def start_table(packed_prompt_length):
    prompt_ends = jnp.cumsum(packed_prompt_length)
    return prompt_ends - packed_prompt_length


def slot_table(prompt_adapter_ids, slot_adapter_ids):
    active_slots = slot_adapter_ids.shape[0]
    matched = slot_adapter_ids[None, :] == prompt_adapter_ids[:, None]
    return jnp.sum(
        jnp.where(matched, jnp.arange(active_slots, dtype=jnp.int32)[None, :], 0), axis=1
    )


def token_prompts(positions, prompt_starts):
    inside = (positions[:, None] >= prompt_starts[None, :]).astype(jnp.int32)
    return jnp.sum(inside, axis=1) - 1


def token_slots(prompts, slot_of):
    prompt_count = slot_of.shape[0]
    onehot = prompts[:, None] == jnp.arange(prompt_count, dtype=jnp.int32)[None, :]
    return jnp.sum(jnp.where(onehot, slot_of[None, :], 0), axis=1)


def down_term(row_block, slots_here, down_cols, active_slots):
    combined_output = jnp.dot(row_block, down_cols, preferred_element_type=jnp.float32)
    combined_output = combined_output.reshape(row_block.shape[0], active_slots, -1)
    pick_slot = slots_here[:, None] == jnp.arange(active_slots, dtype=jnp.int32)[None, :]
    return jnp.sum(jnp.where(pick_slot[:, :, None], combined_output, 0.0), axis=1)


def local(
    normed,
    projection_weight,
    adapter_down_weight,
    adapter_up_weight,
    packed_prompt_length,
    prompt_adapter_ids,
    slot_adapter_ids,
    prompt_page_slots,
):
    col_count = lax.axis_size("col")
    row_count = lax.axis_size("row")
    col_index = lax.axis_index("col")
    my_row = lax.axis_index("row")
    tok_all, width_loc = normed.shape
    tok_blk = tok_all // col_count
    head_column_span = projection_weight.shape[2]
    heads_loc = head_column_span // HEAD_DIM
    active_slots = slot_adapter_ids.shape[0]
    adapter_rank_width = adapter_up_weight.shape[2]
    prompt_starts = start_table(packed_prompt_length)
    slot_of = slot_table(prompt_adapter_ids, slot_adapter_ids)
    block_start = col_index * tok_blk
    mine = block_start + jnp.arange(tok_blk, dtype=jnp.int32)
    mine_prompts = token_prompts(mine, prompt_starts)
    mine_slots = token_slots(mine_prompts, slot_of)
    down_weight_slices = lax.all_to_all(
        adapter_down_weight, "col", split_axis=0, concat_axis=1, tiled=True
    )
    down_cols = down_weight_slices.reshape(width_loc, -1)
    own_rows = lax.all_to_all(normed, "col", split_axis=0, concat_axis=1, tiled=True)
    weight_piece = lax.all_gather(projection_weight, "col", axis=0, tiled=True)
    flat_piece = weight_piece.reshape(weight_piece.shape[0], -1)
    projection_total = jnp.dot(own_rows, flat_piece, preferred_element_type=jnp.float32)
    rows_per = tok_all // row_count
    row_first = my_row * rows_per
    row_positions = row_first + jnp.arange(rows_per, dtype=jnp.int32)
    row_slots = token_slots(token_prompts(row_positions, prompt_starts), slot_of)
    row_part = lax.dynamic_slice_in_dim(normed, row_first, rows_per, 0)
    summed = lax.psum(down_term(row_part, row_slots, down_cols, active_slots), "col")
    down_every = lax.all_gather(summed.astype(jnp.bfloat16), "row", axis=0, tiled=True)
    local_down_output = lax.dynamic_slice_in_dim(down_every, block_start, tok_blk, 0)
    pick_half = (mine_slots[:, None] == jnp.arange(active_slots, dtype=jnp.int32)[None, :]).astype(
        jnp.bfloat16
    )

    def reduced_rank_rows(low_part, slot_membership):
        token_spread = (pick_half[:, :, None] * low_part[:, None, :]).reshape(
            tok_blk, active_slots * adapter_rank_width
        )
        up_weight_table = adapter_up_weight[:, slot_membership].reshape(
            active_slots * adapter_rank_width, head_column_span
        )
        return jnp.dot(token_spread, up_weight_table, preferred_element_type=jnp.float32)

    query_token_rows = (
        projection_total[:, :head_column_span]
        + adapter_scale * reduced_rank_rows(local_down_output[:, :adapter_rank_width], 0)
    ).astype(jnp.bfloat16)
    key_rows = projection_total[:, head_column_span : 2 * head_column_span].astype(jnp.bfloat16)
    value_token_rows = (
        projection_total[:, 2 * head_column_span :]
        + adapter_scale * reduced_rank_rows(local_down_output[:, adapter_rank_width:], 1)
    ).astype(jnp.bfloat16)
    own_kv = jnp.stack([key_rows, value_token_rows], axis=1)
    earlier = [shifted(own_kv, "col", 1)]
    window = jnp.concatenate(earlier[::-1] + [own_kv], axis=0)
    window_len = window.shape[0]
    window_pos = block_start - NEAR * tok_blk + jnp.arange(window_len, dtype=jnp.int32)
    window_prompts = token_prompts(window_pos, prompt_starts)
    allowed = (mine_prompts[:, None] == window_prompts[None, :]) & (
        window_pos[None, :] <= mine[:, None]
    )
    query_heads = query_token_rows.reshape(tok_blk, heads_loc, HEAD_DIM)
    key_heads = window[:, 0].reshape(window_len, heads_loc, HEAD_DIM)
    value_heads = window[:, 1].reshape(window_len, heads_loc, HEAD_DIM)
    score_scale = HEAD_DIM ** (-0.5)
    scores = (
        jnp.einsum("qhd,khd->hqk", query_heads, key_heads, preferred_element_type=jnp.float32)
        * score_scale
    )
    limited = jnp.where(allowed[None], scores, masked_score)
    peak_score = jnp.max(limited, axis=2, keepdims=True)
    weight = jnp.where(allowed[None], jnp.exp(scores - peak_score), 0.0)
    denominator = jnp.sum(weight, axis=2)
    mixed_heads = jnp.einsum(
        "hqk,khd->qhd", weight.astype(jnp.bfloat16), value_heads, preferred_element_type=jnp.float32
    )
    attended = (
        (mixed_heads / jnp.transpose(denominator)[:, :, None])
        .reshape(tok_blk, head_column_span)
        .astype(jnp.bfloat16)
    )
    prev_kv = earlier[0]
    page_window = jnp.concatenate(
        [prev_kv, own_kv, jnp.zeros((PAGE, 2, head_column_span), jnp.bfloat16)], axis=0
    )
    max_pages = prompt_page_slots.shape[1]
    lens_rep = jnp.repeat(packed_prompt_length, max_pages)
    starts_rep = jnp.repeat(prompt_starts, max_pages)
    page_index = jnp.tile(jnp.arange(max_pages, dtype=jnp.int32), packed_prompt_length.shape[0])
    page_rows = jnp.clip(lens_rep - PAGE * page_index, 0, PAGE)
    page_first = starts_rep + PAGE * page_index
    my_slots = col_index * SLOTS_DEV + jnp.arange(SLOTS_DEV, dtype=jnp.int32)
    slot_hit = prompt_page_slots.reshape(-1)[None, :] == my_slots[:, None]
    rows_used = jnp.sum(jnp.where(slot_hit, page_rows[None, :], 0), axis=1)
    first_used = jnp.sum(jnp.where(slot_hit, page_first[None, :], 0), axis=1)
    offset = jnp.clip(first_used - (col_index - 1) * tok_blk, 0, 2 * tok_blk)
    page_lines = jnp.arange(PAGE, dtype=jnp.int32)
    pick_rows = (offset[:, None] + page_lines[None, :]).reshape(-1)
    taken_rows = jnp.take(page_window, pick_rows, axis=0).reshape(
        SLOTS_DEV, PAGE, 2, head_column_span
    )
    live_rows = (page_lines[None, :] < rows_used[:, None])[:, :, None, None]
    kv_pages = jnp.where(live_rows, taken_rows, jnp.zeros_like(taken_rows))
    return (attended, kv_pages)


def solution(mesh):
    placed = (
        P(None, "col"),
        P("col", None, "row"),
        P(None, "col", None),
        P(None, None, None, "row"),
        P(),
        P(),
        P(),
        P(),
    )
    return jax.shard_map(
        local,
        mesh=mesh,
        in_specs=placed,
        out_specs=(P("col", "row"), P("col", None, None, "row")),
        check_vma=False,
    )
```

profile of v0, /device:TPU:6, one launch (start us, length us, event | category | flops | bytes accessed | tf_op | source)
XLA Modules:
  0.0 544.9 jit_solution(5829252045479823222)
XLA Ops:
  7.2 0.0 all-gather.2.cloned.1.call-start
  7.2 0.7 all-gather.2.cloned.1.call-update
  7.9 0.5 broadcast.227
  8.4 1.9 reduce.3
  10.3 0.9 copy.105
  11.3 2.4 reshape.319
  13.7 7.4 %all-to-all-start.1 = ((bf16[16,2,7168]{2,1,0:T(2,128)(2,1)}), bf16[16,2,7168]{2,1,0:T(2,128)(2,1)S(1)}, u32[]{:S(2)}, u32[]{:S(2)}) async-start(bf16[16,2,7168]{2,1,0:T(2,128)(2,1)} %reshape.319), calls=%async_computation.1 | async-start | bytes 917504 | tf_op jit(solution)/shard_map/all_to_all | solution.py:77
  21.1 8.1 %copy.104 = bf16[56,16,8,512]{3,2,0,1:T(8,128)(2,1)} copy(bf16[56,16,8,512]{3,2,1,0:T(8,128)(2,1)} %bitcast.61) | data formatting | bytes 14680064 | tf_op jit(solution)/shard_map/all_to_all | solution.py:81
  29.2 1.7 all-to-all-done.1
  31.0 5.9 %all-to-all-start = ((bf16[16,512,448]{1,2,0:T(8,128)(2,1)}), bf16[16,512,448]{1,2,0:T(8,128)(2,1)}, u32[]{:S(2)}, u32[]{:S(2)}) async-start(bf16[16,512,448]{1,2,0:T(8,128)(2,1)} %bitcast.59), calls=%async_computation | async-start | bytes 14680064 | tf_op jit(solution)/shard_map/all_to_all | solution.py:81
  36.9 0.0 copy-done.5
  36.9 0.1 copy.82
  37.0 0.1 reduce-window.9
  37.1 0.1 reduce
  37.3 0.0 copy-done.7
  37.3 0.0 copy-done.8
  37.3 0.1 select_reduce_fusion.4
  37.4 0.1 convert_reduce_fusion.2
  37.5 0.1 select_reduce_fusion.3
  37.6 0.1 convert_reduce_fusion
  37.7 0.1 select_reduce_fusion.2
  37.9 0.1 fusion.21
  38.0 0.1 subtract_clamp_fusion
  38.1 0.1 fusion.36
  38.1 4.2 reshape.320
  42.4 7.0 %copy.84 = bf16[7168,1,32]{0,2,1:T(8,128)(2,1)S(1)} copy(bf16[7168,1,32]{2,1,0:T(2,128)(2,1)} %reshape.320) | data formatting | bytes 917504 | tf_op jit(solution)/shard_map/all_to_all | solution.py:77
  49.4 0.6 all_to_all.30
  50.0 1.9 select_reduce_fusion.1
  52.0 199.3 %all-reduce.1 = bf16[1024,32]{0,1:T(8,128)(2,1)S(1)} all-reduce(f32[1024,32]{0,1:T(8,128)S(1)} %select_reduce_fusion.1), channel_id=1, replica_groups=mesh['row'=8,'col'=16] {'col'}, use_global_device_ids=true, to_apply=%region_7.8 | all-reduce | flops 32768 | bytes 196608 | tf_op jit(solution)/shard_map/psum | solution.py:90
  251.3 13.7 %all_gather.7 = bf16[8192,32]{0,1:T(8,128)(2,1)S(1)} all-gather(bf16[1024,32]{0,1:T(8,128)(2,1)S(1)} %all-reduce.1), channel_id=1, replica_groups=mesh['row'=8,'col'=16] {'row'}, dimensions={0}, use_global_device_ids=true | all-gather | bytes 589824 | tf_op jit(solution)/shard_map/all_gather | solution.py:91
  265.0 66.0 %all-gather.2.cloned.1.call-done = bf16[7168,3,896]{2,0,1:T(8,128)(2,1)} async-done(((bf16[448,3,896]{2,0,1:T(8,128)(2,1)}), bf16[7168,3,896]{2,0,1:T(8,128)(2,1)}) %all-gather.2.cloned.1.call-update) | async-done | bytes 38535184 | tf_op jit(solution)/shard_map/all_gather | solution.py:82
  331.0 51.4 %copy.81 = bf16[7168,3,896]{0,2,1:T(8,128)(2,1)} copy(bf16[7168,3,896]{2,0,1:T(8,128)(2,1)} %all-gather.2.cloned.1.call-done) | data formatting | bytes 77070336 | tf_op jit(solution)/shard_map/all_gather | solution.py:82
  382.4 0.0 all-to-all-done
  382.4 28.4 %fusion.38 = f32[512,2688]{1,0:T(8,128)} fusion(bf16[512,7168]{0,1:T(8,128)(2,1)} %bitcast.1, bf16[7168,2688]{0,1:T(8,128)(2,1)} %bitcast.58), kind=kOutput, calls=%fused_computation.78 | convolution fusion | flops 19730006016 | bytes 51380224 | tf_op jit(solution)/shard_map/dot_general | solution.py:84
  410.8 1.6 fusion.16
  412.4 2.0 fusion.15
  414.3 1.4 pad_maximum_fusion
  415.8 1.9 collective-permute-start
  417.7 0.1 copy.91
  417.8 0.1 eq.123
  417.9 0.1 add.145
  418.0 0.1 min.20
  418.1 0.2 fusion.24
  418.3 0.1 fusion.25
  418.5 0.1 fusion.28
  418.5 0.1 iota_compare_fusion.4
  418.6 1.3 compare_and_fusion
  419.9 2.0 fusion.10
  421.9 1.5 copy.87
  423.4 41.3 %collective-permute-done = bf16[512,2,896]{2,0,1:T(8,128)(2,1)} collective-permute-done((bf16[512,2,896]{2,0,1:T(8,128)(2,1)}, bf16[512,2,896]{2,0,1:T(8,128)(2,1)}, u32[]{:S(2)}, u32[]{:S(2)}) %collective-permute-start) | collective-permute-done | bytes 1835040 | tf_op jit(solution)/shard_map/ppermute | solution.py:17
  464.7 1.8 maximum_maximum_fusion.1
  466.5 2.1 fusion.35
  468.6 3.8 copy.88
  472.5 3.1 maximum_maximum_fusion
  475.6 0.0 copy-start.3
  475.7 15.3 %copy.92 = bf16[1152,2,896]{2,1,0:T(2,128)(2,1)} copy(bf16[1152,2,896]{2,0,1:T(8,128)(2,1)S(1)} %maximum_maximum_fusion) | data formatting | bytes 8257536 | tf_op jit(solution)/shard_map/concatenate | solution.py:145
  490.9 0.0 copy-done
  490.9 2.4 copy.86
  493.3 0.0 copy-done.4
  493.3 12.7 %fusion.37 = (f32[7,512]{1,0:T(8,128)S(1)}, bf16[7,512,1024]{2,1,0:T(8,128)(2,1)}) fusion(pred[512,1024]{1,0:T(8,128)(4,1)S(1)} %copy-done.4, bf16[512,7,128]{0,2,1:T(8,128)(2,1)S(1)} %bitcast.68, bf16[1024,7,128]{0,2,1:T(8,128)(2,1)} %bitcast.62), kind=kOutput, calls=%fused_computation.77 | convolution fusion | flops 1904739328 | bytes 10631168 | tf_op jit(solution)/shard_map/sub | solution.py:134
  506.0 5.7 %fusion.12 = bf16[512,7,128]{0,2,1:T(8,128)(2,1)S(1)} fusion(bf16[1024,7,128]{0,2,1:T(8,128)(2,1)S(1)} %bitcast.63, bf16[7,512,1024]{2,1,0:T(8,128)(2,1)} %get-tuple-element.29, f32[512,7]{0,1:T(8,128)S(1)} %bitcast.72), kind=kOutput, calls=%fused_computation.25 | convolution fusion | flops 940441600 | bytes 10106880 | tf_op jit(solution)/shard_map/hqk,khd->qhd/dot_general | solution.py:136
  511.7 1.3 copy.93
  513.0 16.6 %gather_fusion = bf16[1280,2,896]{2,1,0:T(2,128)(2,1)} fusion(bf16[1152,2,896]{2,1,0:T(2,128)(2,1)} %copy.92, s32[2048]{0:T(1024)S(1)} %pad_clamp_fusion), kind=kCustom, calls=%fused_computation | custom fusion | bytes 9180160 | tf_op jit(solution)/shard_map/jit(_take)/gather | solution.py:161
  529.6 8.5 %broadcast_select_fusion.1 = bf16[10,128,2,896]{3,2,1,0:T(2,128)(2,1)} fusion(pred[10,128]{1,0:T(8,128)(4,1)S(1)} %iota_compare_fusion.4, bf16[10,128,2,896]{3,2,1,0:T(2,128)(2,1)} %bitcast.60, pred[10,128]{1,0:T(8,128)(4,1)S(1)} %fusion.28), kind=kLoop, calls=%fused_computation.7 | loop fusion | flops 4587520 | bytes 9177600 | tf_op jit(solution)/shard_map/jit(_where)/select_n | solution.py:165
  (28 shorter events, 0.2 us)
Async XLA Ops:
  7.2 323.8 %all-gather.2.cloned.1.call-start = ((), (), s32[]{:S(2)}) async-start(), calls=%async_computation.2 | async-start | bytes 40943616 | tf_op jit(solution)/shard_map/all_gather | solution.py:82
  13.7 17.3 %all-to-all-start.1 = ((bf16[16,2,7168]{2,1,0:T(2,128)(2,1)}), bf16[16,2,7168]{2,1,0:T(2,128)(2,1)S(1)}, u32[]{:S(2)}, u32[]{:S(2)}) async-start(bf16[16,2,7168]{2,1,0:T(2,128)(2,1)} %reshape.319), calls=%async_computation.1 | async-start | bytes 917504 | tf_op jit(solution)/shard_map/all_to_all | solution.py:77
  31.0 5.9 %copy-start.5 = (s32[64]{0:T(128)S(1)}, s32[64]{0:T(128)}, u32[]{:S(2)}) copy-start(s32[64]{0:T(128)} %param.12) | copy-start | bytes 772
  31.0 6.3 %copy-start.7 = (s32[64]{0:T(128)S(1)}, s32[64]{0:T(128)}, u32[]{:S(2)}) copy-start(s32[64]{0:T(128)} %param.13) | copy-start | bytes 772
  31.0 6.3 %copy-start.8 = (s32[16]{0:T(128)S(1)}, s32[16]{0:T(128)}, u32[]{:S(2)}) copy-start(s32[16]{0:T(128)} %param.14) | copy-start | bytes 196
  31.0 7.1 %copy-start.2 = (bf16[16,2,16,896]{3,2,1,0:T(8,128)(2,1)S(1)}, bf16[16,2,16,896]{3,2,1,0:T(8,128)(2,1)}, u32[]{:S(2)}) copy-start(bf16[16,2,16,896]{3,2,1,0:T(8,128)(2,1)} %param.11) | copy-start | bytes 2752516
  31.0 351.4 %all-to-all-start = ((bf16[16,512,448]{1,2,0:T(8,128)(2,1)}), bf16[16,512,448]{1,2,0:T(8,128)(2,1)}, u32[]{:S(2)}, u32[]{:S(2)}) async-start(bf16[16,512,448]{1,2,0:T(8,128)(2,1)} %bitcast.59), calls=%async_computation | async-start | bytes 14680064 | tf_op jit(solution)/shard_map/all_to_all | solution.py:81
  410.8 6.9 %copy-start.6 = (s32[64,4]{0,1:T(4,128)S(1)}, s32[64,4]{0,1:T(4,128)}, u32[]{:S(2)}) copy-start(s32[64,4]{0,1:T(4,128)} %param.15) | copy-start | bytes 3076
  415.8 49.0 %collective-permute-start = (bf16[512,2,896]{2,0,1:T(8,128)(2,1)}, bf16[512,2,896]{2,0,1:T(8,128)(2,1)}, u32[]{:S(2)}, u32[]{:S(2)}) collective-permute-start(bf16[512,2,896]{2,0,1:T(8,128)(2,1)} %pad_maximum_fusion), channel_id=1, source_target_pairs={{0,1},{1,2},{2,3},{3,4},{4,5},{5,6},{6,7},{7,8},{8,9},{9,10},{10,1... | collective-permute-start | bytes 5505032 | tf_op jit(solution)/shard_map/ppermute | solution.py:17
  475.6 15.3 %copy-start = (bf16[1024,1,896]{2,0,1:T(8,128)(2,1)S(1)}, bf16[1024,1,896]{2,0,1:T(8,128)(2,1)}, u32[]{:S(2)}) copy-start(bf16[1024,1,896]{2,0,1:T(8,128)(2,1)} %get-tuple-element.21) | copy-start | bytes 5505028
  475.6 17.7 %copy-start.3 = (bf16[512,896]{0,1:T(8,128)(2,1)S(1)}, bf16[512,896]{0,1:T(8,128)(2,1)}, u32[]{:S(2)}) copy-start(bf16[512,896]{0,1:T(8,128)(2,1)} %copy.87) | copy-start | bytes 2752516
  475.6 17.7 %copy-start.4 = (pred[512,1024]{1,0:T(8,128)(4,1)S(1)}, pred[512,1024]{1,0:T(8,128)(4,1)}, u32[]{:S(2)}) copy-start(pred[512,1024]{1,0:T(8,128)(4,1)} %compare_and_fusion) | copy-start | bytes 1572868
  493.3 12.7 %copy-start.1 = (bf16[1024,1,896]{0,2,1:T(8,128)(2,1)S(1)}, bf16[1024,1,896]{0,2,1:T(8,128)(2,1)}, u32[]{:S(2)}) copy-start(bf16[1024,1,896]{0,2,1:T(8,128)(2,1)} %copy.86) | copy-start | bytes 5505028
Sparse Core Ops, SparseCore 0:
  10.1 320.8 all-gather.1
where the time goes:
time: 547 us; the launch traced here: 545 us
  blocking collectives  213 us (39%)
  local copies, waits for them, and re-layouts  120 us (22%)
  waiting for transfers between devices  110 us (20%)
  matrix products  52.6 us (10%)
  other arithmetic  19.5 us (4%)
  starting transfers between devices  15.3 us (3%)
  between operations  14.3 us (3%)
    psum x1, blocking collectives, local(): lax.psum(down_term(row_part, row_slots, down_cols, active_slots), 'col')  199 us
    all_gather x1, waiting for transfers between devices, local(): weight_piece = lax.all_gather(projection_weight, 'col', axis=0, tiled=True)  66 us
    all_gather x1, local copies, waits for them, and re-layouts, local(): weight_piece = lax.all_gather(projection_weight, 'col', axis=0, tiled=True)  51.4 us
    ppermute x1, waiting for transfers between devices, shifted(): return lax.ppermute(block, axis, route)  41.3 us
    dot_general x1, matrix products, local(): jnp.dot(own_rows, flat_piece, preferred_element_type=jnp.float32)  28.4 us
    gather x1, local copies, waits for them, and re-layouts, local(): jnp.take(page_window, pick_rows, axis=0)  16.6 us
    concatenate x2, local copies, waits for them, and re-layouts, local(): jnp.concatenate([prev_kv, own_kv, jnp.zeros((PAGE, 2, head_column_span),...  15.3 us
    all_gather x1, blocking collectives, local(): lax.all_gather(summed.astype(jnp.bfloat16), 'row', axis=0, tiled=True)  13.7 us
  transfers between devices with their start and end apart: 4, of which 3 were waited for; matrix products, arithmetic and copies ran while one was open for 16% of the time, Pallas kernels for 0%

commit v1 on v0

--- a/solution.py
+++ b/solution.py
@@ -1,7 +1,9 @@
+import functools
 import jax
 import jax.numpy as jnp
 from jax import lax
 from jax.sharding import PartitionSpec as P
+from jax.lax import axis_index, axis_size, ppermute
 
 HEAD_DIM = 128
 PAGE = 128
@@ -9,6 +11,30 @@
 SLOTS_DEV = 10
 adapter_scale = 2.0
 masked_score = -1e30
+
+
+def _direct_classes(arr_in, device_axis):
+    w1, clean, heard = (axis_size(device_axis), axis_index(device_axis), arr_in.shape[0])
+    chunks = list(map(lambda u: (u, (u + 1) % w1), range(w1)))
+    cards = list(map(lambda u: (u, (u - 1) % w1), range(w1)))
+    outcome_arr = jnp.zeros((*arr_in.shape[:0], w1 * heard, *arr_in.shape[1:]), arr_in.dtype)
+    outcome_arr = lax.dynamic_update_slice_in_dim(outcome_arr, arr_in, clean * heard, axis=0)
+    spare = w1 // 2
+    u1 = left_arr = arr_in
+    for p in range(1, spare + 1):
+        u1 = ppermute(u1, device_axis, chunks)
+        outcome_arr = lax.dynamic_update_slice_in_dim(
+            outcome_arr, u1, (clean - p) % w1 * heard, axis=0
+        )
+        if p < w1 - spare:
+            left_arr = ppermute(left_arr, device_axis, cards)
+            outcome_arr = lax.dynamic_update_slice_in_dim(
+                outcome_arr, left_arr, (clean + p) % w1 * heard, axis=0
+            )
+    return outcome_arr
+
+
+create_the_paths = functools.partial(_direct_classes, device_axis="row")
 
 
 def shifted(block, axis, distance):
@@ -88,7 +114,7 @@
     row_slots = token_slots(token_prompts(row_positions, prompt_starts), slot_of)
     row_part = lax.dynamic_slice_in_dim(normed, row_first, rows_per, 0)
     summed = lax.psum(down_term(row_part, row_slots, down_cols, active_slots), "col")
-    down_every = lax.all_gather(summed.astype(jnp.bfloat16), "row", axis=0, tiled=True)
+    down_every = create_the_paths(summed.astype(jnp.bfloat16))
     local_down_output = lax.dynamic_slice_in_dim(down_every, block_start, tok_blk, 0)
     pick_half = (mine_slots[:, None] == jnp.arange(active_slots, dtype=jnp.int32)[None, :]).astype(
         jnp.bfloat16

time: 547 us -> 547 us (level)
  blocking collectives: 213 us -> 199 us
  starting transfers between devices: 15.3 us -> 25.2 us
    all_gather x1 -> x0, blocking collectives: 13.7 us -> none  [local(): lax.all_gather(summed.astype(jnp.bfloat16), 'row', axis=0, tiled=True)]
    ppermute x0 -> x7, waiting for transfers between devices: none -> 9.74 us  [the longest x4 8.64 us: _direct_classes(): u1 = ppermute(u1, device_axis, chunks)]
    ppermute x0 -> x7, starting transfers between devices: none -> 9.71 us  [the longest x3 9.69 us: _direct_classes(): left_arr = ppermute(left_arr, device_axis, cards)]
    all_gather x1, waiting for transfers between devices: 66 us -> 60 us  [local(): weight_piece = lax.all_gather(projection_weight, 'col', axis=0, tiled=True)]
  transfers between devices with their start and end apart: 4 -> 11, of which waited for: 3 -> 9; matrix products, arithmetic and copies ran while one was open for 16% -> 16% of each run, Pallas kernels for 0% -> 0%
where the time goes in v1:
time: 547 us; the launch traced here: 545 us
  blocking collectives  199 us (36%)
  local copies, waits for them, and re-layouts  120 us (22%)
  waiting for transfers between devices  114 us (21%)
  matrix products  52.6 us (10%)
  starting transfers between devices  25.2 us (5%)
  other arithmetic  19.5 us (4%)
  between operations  14.4 us (3%)
    psum x1, blocking collectives, local(): lax.psum(down_term(row_part, row_slots, down_cols, active_slots), 'col')  199 us
    all_gather x1, waiting for transfers between devices, local(): weight_piece = lax.all_gather(projection_weight, 'col', axis=0, tiled=True)  60 us
    all_gather x1, local copies, waits for them, and re-layouts, local(): weight_piece = lax.all_gather(projection_weight, 'col', axis=0, tiled=True)  51.4 us
    ppermute x1, waiting for transfers between devices, shifted(): return lax.ppermute(block, axis, route)  41.4 us
    dot_general x1, matrix products, local(): jnp.dot(own_rows, flat_piece, preferred_element_type=jnp.float32)  28.4 us
    gather x1, local copies, waits for them, and re-layouts, local(): jnp.take(page_window, pick_rows, axis=0)  16.5 us
    concatenate x2, local copies, waits for them, and re-layouts, local(): jnp.concatenate([prev_kv, own_kv, jnp.zeros((PAGE, 2, head_column_span),...  15.3 us
    sub x1, matrix products, local(): weight = jnp.where(allowed[None], jnp.exp(scores - peak_score), 0.0)  12.7 us
  transfers between devices with their start and end apart: 11, of which 9 were waited for; matrix products, arithmetic and copies ran while one was open for 16% of the time, Pallas kernels for 0%

profile of v1, /device:TPU:6, one launch (start us, length us, event | category | flops | bytes accessed | tf_op | source)
XLA Modules:
  0.0 544.8 jit_solution(1952589002538246852)
XLA Ops:
  7.2 0.7 all-gather.2.cloned.1.call-update
  7.9 0.5 broadcast.234
  8.4 1.9 reduce.3
  10.3 0.9 copy.105
  11.3 2.4 reshape.319
  13.7 7.4 %all-to-all-start.1 = ((bf16[16,2,7168]{2,1,0:T(2,128)(2,1)}), bf16[16,2,7168]{2,1,0:T(2,128)(2,1)S(1)}, u32[]{:S(2)}, u32[]{:S(2)}) async-start(bf16[16,2,7168]{2,1,0:T(2,128)(2,1)} %reshape.319), calls=%async_computation.1 | async-start | bytes 917504 | tf_op jit(solution)/shard_map/all_to_all | solution.py:103
  21.1 8.1 %copy.104 = bf16[56,16,8,512]{3,2,0,1:T(8,128)(2,1)} copy(bf16[56,16,8,512]{3,2,1,0:T(8,128)(2,1)} %bitcast.61) | data formatting | bytes 14680064 | tf_op jit(solution)/shard_map/all_to_all | solution.py:107
  29.2 1.7 all-to-all-done.1
  31.0 5.9 %all-to-all-start = ((bf16[16,512,448]{1,2,0:T(8,128)(2,1)}), bf16[16,512,448]{1,2,0:T(8,128)(2,1)}, u32[]{:S(2)}, u32[]{:S(2)}) async-start(bf16[16,512,448]{1,2,0:T(8,128)(2,1)} %bitcast.59), calls=%async_computation | async-start | bytes 14680064 | tf_op jit(solution)/shard_map/all_to_all | solution.py:107
  36.9 0.1 copy.82
  37.0 0.1 reduce-window.9
  37.1 0.1 reduce
  37.3 0.1 select_reduce_fusion.4
  37.4 0.1 convert_reduce_fusion.2
  37.5 0.1 select_reduce_fusion.3
  37.6 0.1 convert_reduce_fusion
  37.8 0.1 select_reduce_fusion.2
  37.9 0.1 fusion.21
  38.0 0.1 subtract_clamp_fusion
  38.1 0.1 fusion.36
  38.2 4.2 reshape.320
  42.4 7.0 %copy.84 = bf16[7168,1,32]{0,2,1:T(8,128)(2,1)S(1)} copy(bf16[7168,1,32]{2,1,0:T(2,128)(2,1)} %reshape.320) | data formatting | bytes 917504 | tf_op jit(solution)/shard_map/all_to_all | solution.py:103
  49.4 0.6 all_to_all.30
  50.1 1.9 select_reduce_fusion.1
  52.0 199.3 %all-reduce.1 = bf16[1024,32]{0,1:T(8,128)(2,1)S(1)} all-reduce(f32[1024,32]{0,1:T(8,128)S(1)} %select_reduce_fusion.1), channel_id=1, replica_groups=mesh['row'=8,'col'=16] {'col'}, use_global_device_ids=true, to_apply=%region_7.8 | all-reduce | flops 32768 | bytes 196608 | tf_op jit(solution)/shard_map/psum | solution.py:116
  251.3 2.9 collective-permute-start.1
  254.3 1.9 collective-permute-done
  256.2 3.4 collective-permute-start.3
  259.6 1.5 collective-permute-done.2
  261.1 0.4 collective-permute-done.3
  261.4 3.4 collective-permute-start.5
  264.9 1.1 collective-permute-done.4
  266.0 0.7 collective-permute-done.5
  266.8 4.1 collective-permute-done.6
  271.0 60.0 %all-gather.2.cloned.1.call-done = bf16[7168,3,896]{2,0,1:T(8,128)(2,1)} async-done(((bf16[448,3,896]{2,0,1:T(8,128)(2,1)}), bf16[7168,3,896]{2,0,1:T(8,128)(2,1)}) %all-gather.2.cloned.1.call-update) | async-done | bytes 38535184 | tf_op jit(solution)/shard_map/all_gather | solution.py:108
  331.0 51.4 %copy.81 = bf16[7168,3,896]{0,2,1:T(8,128)(2,1)} copy(bf16[7168,3,896]{2,0,1:T(8,128)(2,1)} %all-gather.2.cloned.1.call-done) | data formatting | bytes 77070336 | tf_op jit(solution)/shard_map/all_gather | solution.py:108
  382.4 28.4 %fusion.38 = f32[512,2688]{1,0:T(8,128)} fusion(bf16[512,7168]{0,1:T(8,128)(2,1)} %bitcast.1, bf16[7168,2688]{0,1:T(8,128)(2,1)} %bitcast.58), kind=kOutput, calls=%fused_computation.86 | convolution fusion | flops 19730006016 | bytes 51380224 | tf_op jit(solution)/shard_map/dot_general | solution.py:110
  410.8 1.6 fusion.16
  412.4 2.0 fusion.15
  414.3 1.4 pad_maximum_fusion
  415.8 2.1 collective-permute-start.7
  417.9 0.1 copy.91
  418.0 0.1 eq.131
  418.1 0.1 add.219
  418.2 0.1 min.20
  418.3 0.2 fusion.24
  418.5 0.1 fusion.25
  418.6 0.1 fusion.28
  418.7 0.1 iota_compare_fusion.4
  418.8 1.3 compare_and_fusion
  420.1 2.0 fusion.10
  422.1 1.3 copy.87
  423.3 41.4 %collective-permute-done.7 = bf16[512,2,896]{2,0,1:T(8,128)(2,1)} collective-permute-done((bf16[512,2,896]{2,0,1:T(8,128)(2,1)}, bf16[512,2,896]{2,0,1:T(8,128)(2,1)}, u32[]{:S(2)}, u32[]{:S(2)}) %collective-permute-start.7) | collective-permute-done | bytes 1835040 | tf_op jit(solution)/shard_map/ppermute | solution.py:43
  464.7 1.8 maximum_maximum_fusion.1
  466.5 2.1 fusion.35
  468.6 3.8 copy.88
  472.5 3.1 maximum_maximum_fusion
  475.7 15.3 %copy.92 = bf16[1152,2,896]{2,1,0:T(2,128)(2,1)} copy(bf16[1152,2,896]{2,0,1:T(8,128)(2,1)S(1)} %maximum_maximum_fusion) | data formatting | bytes 8257536 | tf_op jit(solution)/shard_map/concatenate | solution.py:171
  490.9 2.4 copy.86
  493.3 12.7 %fusion.37 = (f32[7,512]{1,0:T(8,128)S(1)}, bf16[7,512,1024]{2,1,0:T(8,128)(2,1)}) fusion(pred[512,1024]{1,0:T(8,128)(4,1)S(1)} %copy-done.4, bf16[512,7,128]{0,2,1:T(8,128)(2,1)S(1)} %bitcast.68, bf16[1024,7,128]{0,2,1:T(8,128)(2,1)} %bitcast.62), kind=kOutput, calls=%fused_computation.85 | convolution fusion | flops 1904739328 | bytes 10631168 | tf_op jit(solution)/shard_map/sub | solution.py:160
  506.0 5.7 %fusion.12 = bf16[512,7,128]{0,2,1:T(8,128)(2,1)S(1)} fusion(bf16[1024,7,128]{0,2,1:T(8,128)(2,1)S(1)} %bitcast.63, bf16[7,512,1024]{2,1,0:T(8,128)(2,1)} %get-tuple-element.29, f32[512,7]{0,1:T(8,128)S(1)} %bitcast.72), kind=kOutput, calls=%fused_computation.25 | convolution fusion | flops 940441600 | bytes 10106880 | tf_op jit(solution)/shard_map/hqk,khd->qhd/dot_general | solution.py:162
  511.7 1.3 copy.93
  513.0 16.5 %gather_fusion = bf16[1280,2,896]{2,1,0:T(2,128)(2,1)} fusion(bf16[1152,2,896]{2,1,0:T(2,128)(2,1)} %copy.92, s32[2048]{0:T(1024)S(1)} %pad_clamp_fusion), kind=kCustom, calls=%fused_computation | custom fusion | bytes 9180160 | tf_op jit(solution)/shard_map/jit(_take)/gather | solution.py:187
  529.5 8.5 %broadcast_select_fusion.1 = bf16[10,128,2,896]{3,2,1,0:T(2,128)(2,1)} fusion(pred[10,128]{1,0:T(8,128)(4,1)S(1)} %iota_compare_fusion.4, bf16[10,128,2,896]{3,2,1,0:T(2,128)(2,1)} %bitcast.60, pred[10,128]{1,0:T(8,128)(4,1)S(1)} %fusion.28), kind=kLoop, calls=%fused_computation.7 | loop fusion | flops 4587520 | bytes 9177600 | tf_op jit(solution)/shard_map/jit(_where)/select_n | solution.py:191
  (50 shorter events, 0.4 us)
Async XLA Ops:
  7.2 323.8 %all-gather.2.cloned.1.call-start = ((), (), s32[]{:S(2)}) async-start(), calls=%async_computation.2 | async-start | bytes 40943616 | tf_op jit(solution)/shard_map/all_gather | solution.py:108
  13.7 17.3 %all-to-all-start.1 = ((bf16[16,2,7168]{2,1,0:T(2,128)(2,1)}), bf16[16,2,7168]{2,1,0:T(2,128)(2,1)S(1)}, u32[]{:S(2)}, u32[]{:S(2)}) async-start(bf16[16,2,7168]{2,1,0:T(2,128)(2,1)} %reshape.319), calls=%async_computation.1 | async-start | bytes 917504 | tf_op jit(solution)/shard_map/all_to_all | solution.py:103
  31.0 5.9 %copy-start.5 = (s32[64]{0:T(128)S(1)}, s32[64]{0:T(128)}, u32[]{:S(2)}) copy-start(s32[64]{0:T(128)} %param.12) | copy-start | bytes 772
  31.0 6.3 %copy-start.7 = (s32[64]{0:T(128)S(1)}, s32[64]{0:T(128)}, u32[]{:S(2)}) copy-start(s32[64]{0:T(128)} %param.13) | copy-start | bytes 772
  31.0 6.3 %copy-start.8 = (s32[16]{0:T(128)S(1)}, s32[16]{0:T(128)}, u32[]{:S(2)}) copy-start(s32[16]{0:T(128)} %param.14) | copy-start | bytes 196
  31.0 7.1 %copy-start.2 = (bf16[16,2,16,896]{3,2,1,0:T(8,128)(2,1)S(1)}, bf16[16,2,16,896]{3,2,1,0:T(8,128)(2,1)}, u32[]{:S(2)}) copy-start(bf16[16,2,16,896]{3,2,1,0:T(8,128)(2,1)} %param.11) | copy-start | bytes 2752516
  31.0 351.4 %all-to-all-start = ((bf16[16,512,448]{1,2,0:T(8,128)(2,1)}), bf16[16,512,448]{1,2,0:T(8,128)(2,1)}, u32[]{:S(2)}, u32[]{:S(2)}) async-start(bf16[16,512,448]{1,2,0:T(8,128)(2,1)} %bitcast.59), calls=%async_computation | async-start | bytes 14680064 | tf_op jit(solution)/shard_map/all_to_all | solution.py:107
  251.3 4.9 collective-permute-start
  251.3 4.9 collective-permute-start.1
  256.2 4.9 collective-permute-start.2
  256.2 5.3 collective-permute-start.3
  261.1 4.9 collective-permute-start.4
  261.4 5.3 collective-permute-start.5
  266.0 4.9 collective-permute-start.6
  410.8 7.1 %copy-start.6 = (s32[64,4]{0,1:T(4,128)S(1)}, s32[64,4]{0,1:T(4,128)}, u32[]{:S(2)}) copy-start(s32[64,4]{0,1:T(4,128)} %param.15) | copy-start | bytes 3076
  415.8 49.0 %collective-permute-start.7 = (bf16[512,2,896]{2,0,1:T(8,128)(2,1)}, bf16[512,2,896]{2,0,1:T(8,128)(2,1)}, u32[]{:S(2)}, u32[]{:S(2)}) collective-permute-start(bf16[512,2,896]{2,0,1:T(8,128)(2,1)} %pad_maximum_fusion), channel_id=1, source_target_pairs={{0,1},{1,2},{2,3},{3,4},{4,5},{5,6},{6,7},{7,8},{8,9},{9,10},{10,1... | collective-permute-start | bytes 5505032 | tf_op jit(solution)/shard_map/ppermute | solution.py:43
  475.6 15.3 %copy-start = (bf16[1024,1,896]{2,0,1:T(8,128)(2,1)S(1)}, bf16[1024,1,896]{2,0,1:T(8,128)(2,1)}, u32[]{:S(2)}) copy-start(bf16[1024,1,896]{2,0,1:T(8,128)(2,1)} %get-tuple-element.21) | copy-start | bytes 5505028
  475.6 17.7 %copy-start.3 = (bf16[512,896]{0,1:T(8,128)(2,1)S(1)}, bf16[512,896]{0,1:T(8,128)(2,1)}, u32[]{:S(2)}) copy-start(bf16[512,896]{0,1:T(8,128)(2,1)} %copy.87) | copy-start | bytes 2752516
  475.6 17.7 %copy-start.4 = (pred[512,1024]{1,0:T(8,128)(4,1)S(1)}, pred[512,1024]{1,0:T(8,128)(4,1)}, u32[]{:S(2)}) copy-start(pred[512,1024]{1,0:T(8,128)(4,1)} %compare_and_fusion) | copy-start | bytes 1572868
  493.3 12.7 %copy-start.1 = (bf16[1024,1,896]{0,2,1:T(8,128)(2,1)S(1)}, bf16[1024,1,896]{0,2,1:T(8,128)(2,1)}, u32[]{:S(2)}) copy-start(bf16[1024,1,896]{0,2,1:T(8,128)(2,1)} %copy.86) | copy-start | bytes 5505028
Sparse Core Ops, SparseCore 0:
  10.1 320.8 all-gather.1
